TPU v7x, 32 devices: a whole 2x2x4 slice. The times are simulated.
32 devices in a mesh: ctx: 8 (over z, core), head: 4 (over y, x).
Axes of the slice: x: 2, y: 2, z: 4, core: 2. Of those that a mesh axis runs over, the one named last changes fastest.
Arguments:
- query: bfloat16 [4096, 64, 128], P('ctx', 'head'), may hold values from -8 to 8
- keys: bfloat16 [4096, 8, 128], P('ctx', 'head'), may hold values from -8 to 8
- values: bfloat16 [4096, 8, 128], P('ctx', 'head'), may hold values from -6 to 6
- k_scale: bfloat16 [16, 8], P('ctx', 'head'), may hold values from 0.59765625 to 1.59375
- v_scale: bfloat16 [16, 8], P('ctx', 'head'), may hold values from 0.5 to 2
- block_place: int32 [16], P('ctx'), may hold values from 0 to 15, as said below
- out_weight: bfloat16 [8192, 8192], P('head'), may hold values from -1 to 1
Outputs:
- mixed: bfloat16 [4096, 8192], P(('ctx', 'head'))
Inputs may be any that keep to these rules, and one draw needn't show every extreme that they name: `block_place`: A permutation of the block indices in which entries 2r and 2r + 1 sum to 15 and entry 2r is below 8.
All inputs are finite; a program needn't handle non-finite values.
Results may differ from a plain program's by a relative error of at most 0.015.
Values may be sent and summed in bfloat16 or wider, within the bound.
A program may use at most 128 MiB of HBM per device.

v0:
```python
import functools
import math

import jax
import jax.numpy as jnp
from jax import lax
from jax.experimental import pallas as pl
from jax.experimental.pallas import tpu as pltpu
from jax.sharding import PartitionSpec as P

masked_value = -1e30
COLUMN_CHUNKS = 4


def attend_kernel(
    per_group, block_len, head_dim, blocks,
    order, own, key_gain, value_gain,
    q_ref, k_ref, vt_ref, o_ref,
    max_ref, total_ref, sum_ref,
):
    group = pl.program_id(0)
    place = own[pl.program_id(1)]

    def tile(index, first):
        block = order[index]
        owner = lax.div(block, 2)
        start = pl.multiple_of(lax.rem(block, 2) * block_len, block_len)
        key = k_ref[owner, pl.ds(start, block_len), :]
        value_t = vt_ref[owner, :, pl.ds(start, block_len)]
        gain = key_gain[group * blocks + block]
        scale = value_gain[group * blocks + block]
        if first:
            shape = (block_len, block_len)
            visible = lax.broadcasted_iota(jnp.int32, shape, 0) <= lax.broadcasted_iota(
                jnp.int32, shape, 1
            )
        for h in range(per_group):
            columns = slice(h * head_dim, (h + 1) * head_dim)
            scores = lax.dot_general(
                key, q_ref[:, columns], (((1,), (1,)), ((), ())),
                preferred_element_type=jnp.float32,
            )
            if first:
                scores = jnp.where(visible, scores, masked_value)
            top = jnp.max(scores, axis=0, keepdims=True) * gain
            if not first:
                old = max_ref[h : h + 1, :]
                top = jnp.maximum(old, top)
            weights = jnp.exp2(scores * gain - top)
            total = jnp.sum(weights, axis=0, keepdims=True)
            product = lax.dot_general(
                value_t, weights.astype(jnp.bfloat16), (((1,), (0,)), ((), ())),
                preferred_element_type=jnp.float32,
            ) * scale
            if not first:
                factor = jnp.exp2(old - top)
                total = total + factor * total_ref[h : h + 1, :]
                product = product + factor * sum_ref[h]
            max_ref[h : h + 1, :] = top
            total_ref[h : h + 1, :] = total
            sum_ref[h] = product

    tile(place, True)

    @pl.loop(0, place)
    def _(index):
        tile(index, False)

    for h in range(per_group):
        columns = slice(h * head_dim, (h + 1) * head_dim)
        mean = sum_ref[h] / total_ref[h : h + 1, :]
        o_ref[:, columns] = mean.T.astype(o_ref.dtype)


def attend(order, own, key_gain, value_gain, query, keys, values_t, group_count):
    rows, width = query.shape
    devices, _, key_width = keys.shape
    head_dim = key_width // group_count
    slots = own.shape[0]
    block_len = rows // slots
    group_width = width // group_count
    per_group = group_width // head_dim
    blocks = order.shape[0]
    pairs = slots * block_len * rows * devices * per_group * group_count // 2
    return pl.pallas_call(
        functools.partial(attend_kernel, per_group, block_len, head_dim, blocks),
        grid_spec=pltpu.PrefetchScalarGridSpec(
            num_scalar_prefetch=4,
            grid=(group_count, slots),
            in_specs=[
                pl.BlockSpec((block_len, group_width), lambda g, s, *_: (s, g)),
                pl.BlockSpec((devices, rows, head_dim), lambda g, s, *_: (0, 0, g)),
                pl.BlockSpec((devices, head_dim, rows), lambda g, s, *_: (0, g, 0)),
            ],
            out_specs=pl.BlockSpec((block_len, group_width), lambda g, s, *_: (s, g)),
            scratch_shapes=[
                pltpu.VMEM((per_group, block_len), jnp.float32),
                pltpu.VMEM((per_group, block_len), jnp.float32),
                pltpu.VMEM((per_group, head_dim, block_len), jnp.float32),
            ],
        ),
        out_shape=jax.ShapeDtypeStruct((rows, width), jnp.bfloat16),
        compiler_params=pltpu.CompilerParams(vmem_limit_bytes=50 * 1024 * 1024),
        cost_estimate=pl.CostEstimate(
            flops=4 * pairs * head_dim, bytes_accessed=8 << 20, transcendentals=pairs
        ),
    )(order, own, key_gain, value_gain, query, keys, values_t)


def body(query, keys, values, k_scale, v_scale, block_place, out_weight):
    rows, head_count, head_dim = query.shape
    group_count = keys.shape[1]
    slots = block_place.shape[0]
    devices = lax.axis_size("ctx")
    blocks = slots * devices
    width = group_count * head_dim
    facts = jnp.concatenate(
        [k_scale, v_scale, block_place[:, None].astype(jnp.bfloat16)], axis=1
    )
    facts = jnp.pad(facts, ((0, 16 - slots), (0, width - facts.shape[1])))
    key_part = jnp.concatenate([keys.reshape(rows, width), facts], axis=0)
    all_keys = lax.all_gather(key_part, "ctx", axis=0, tiled=False)
    all_values = lax.all_gather(values.reshape(rows, width).T, "ctx", axis=0, tiled=False)
    all_facts = all_keys[:, rows : rows + slots, : 2 * group_count + 1].reshape(blocks, -1)
    all_facts = all_facts.astype(jnp.float32)
    places = all_facts[:, -1].astype(jnp.int32)
    ids = jnp.arange(blocks, dtype=jnp.int32)
    order = jnp.sum(jnp.where(places[None, :] == ids[:, None], ids[None, :], 0), axis=1)
    rate = math.log2(math.e) / math.sqrt(head_dim)
    key_gain = (all_facts[:, :group_count] * rate).T.reshape(-1)
    value_gain = all_facts[:, group_count : 2 * group_count].T.reshape(-1)
    attended = attend(
        order, block_place, key_gain, value_gain,
        query.reshape(rows, head_count * head_dim), all_keys[:, :rows], all_values, group_count,
    )
    step = out_weight.shape[1] // COLUMN_CHUNKS
    pieces = []
    for c in range(COLUMN_CHUNKS):
        term = jnp.dot(
            attended, out_weight[:, c * step : (c + 1) * step],
            preferred_element_type=jnp.float32,
        ).astype(jnp.bfloat16)
        pieces.append(lax.psum_scatter(term, "head", scatter_dimension=0, tiled=True))
    return jnp.concatenate(pieces, axis=1)


def solution(mesh):
    placed = (
        P("ctx", "head", None),
        P("ctx", "head", None),
        P("ctx", "head", None),
        P("ctx", "head"),
        P("ctx", "head"),
        P("ctx"),
        P("head", None),
    )
    return jax.shard_map(
        body, mesh=mesh, in_specs=placed, out_specs=P(("ctx", "head"), None), check_vma=False
    )
```

profile of v0, /device:TPU:0, one launch (start us, length us, event | category | flops | bytes accessed | tf_op | source)
XLA Modules:
  0.0 324.8 jit_solution(4033587526142610872)
XLA Ops:
  6.5 0.8 convert_bitcast_fusion
  7.3 0.1 copy.16
  7.5 1.0 copy.26
  8.4 0.8 fusion.28
  9.2 0.7 pad_maximum_fusion.1
  10.0 1.8 copy.20
  11.9 1.9 copy.25
  13.7 28.8 %all-gather.5.cloned.1.call-done = bf16[4224,256]{1,0:T(8,128)(2,1)} async-done(((bf16[528,256]{1,0:T(8,128)(2,1)}), bf16[4224,256]{1,0:T(8,128)(2,1)}) %all-gather.5.cloned.1.call-update) | async-done | bytes 2162704 | tf_op jit(solution)/shard_map/all_gather | solution.py:122
  42.5 0.7 slice.36
  43.2 3.1 slice.40.k_ref
  46.5 0.1 reshape.27.value_gain
  46.7 0.2 fusion.30
  46.9 0.1 select_reduce_fusion.order
  47.0 25.7 %all-gather.7.cloned.1.call-done = bf16[2048,512]{1,0:T(8,128)(2,1)} async-done(((bf16[256,512]{1,0:T(8,128)(2,1)}), bf16[2048,512]{1,0:T(8,128)(2,1)}) %all-gather.7.cloned.1.call-update) | async-done | bytes 2097168 | tf_op jit(solution)/shard_map/all_gather | solution.py:123
  72.7 84.1 %shard_map.73 = bf16[512,2048]{1,0:T(8,128)(2,1)S(1)} custom-call(s32[16]{0:T(128)S(1)} %select_reduce_fusion.order, s32[2]{0:T(128)S(1)} %copy-done, f32[32]{0:T(128)S(1)} %reshape.26.key_gain, f32[32]{0:T(128)S(1)} %reshape.27.value_gain, bf16[512,2048]{1,0:T(8,128)(2,1)} %bitcast.26, bf16[8,512,256]{2,1,0:T(8,128)(2,1)} %slice.40.k_ref, ...), custom_call_target="tpu_custom_call" | custom-call | flops 8589934592 | bytes 8388608 | tf_op jit(solution)/shard_map/pallas_call | solution.py:85
  156.8 9.0 %fusion.17 = bf16[512,2048]{1,0:T(8,128)(2,1)} fusion(bf16[512,2048]{1,0:T(8,128)(2,1)S(1)} %shard_map.73, bf16[2048,8192]{1,0:T(8,128)(2,1)} %param.13), kind=kOutput, calls=%fused_computation.11 | convolution fusion | flops 4296015872 | bytes 12582912 | tf_op jit(solution)/shard_map/dot_general | solution.py:139
  165.9 9.1 %fusion.14 = bf16[512,2048]{1,0:T(8,128)(2,1)} fusion(bf16[512,2048]{1,0:T(8,128)(2,1)S(1)} %shard_map.73, bf16[2048,8192]{1,0:T(8,128)(2,1)} %param.13), kind=kOutput, calls=%fused_computation.10 | convolution fusion | flops 4296015872 | bytes 12582912 | tf_op jit(solution)/shard_map/dot_general | solution.py:139
  175.1 9.2 %fusion.8 = bf16[512,2048]{1,0:T(8,128)(2,1)} fusion(bf16[512,2048]{1,0:T(8,128)(2,1)S(1)} %shard_map.73, bf16[2048,8192]{1,0:T(8,128)(2,1)} %param.13), kind=kOutput, calls=%fused_computation.8 | convolution fusion | flops 4296015872 | bytes 12582912 | tf_op jit(solution)/shard_map/dot_general | solution.py:139
  184.4 9.2 %fusion.11 = bf16[512,2048]{1,0:T(8,128)(2,1)} fusion(bf16[512,2048]{1,0:T(8,128)(2,1)S(1)} %shard_map.73, bf16[2048,8192]{1,0:T(8,128)(2,1)} %param.13), kind=kOutput, calls=%fused_computation.9 | convolution fusion | flops 4296015872 | bytes 12582912 | tf_op jit(solution)/shard_map/dot_general | solution.py:139
  193.6 7.2 %reduce-scatter.11.cloned.1.call-done = bf16[128,2048]{1,0:T(8,128)(2,1)} async-done(((bf16[512,2048]{1,0:T(8,128)(2,1)}), bf16[128,2048]{1,0:T(8,128)(2,1)}) %reduce-scatter.11.cloned.1.call-update) | async-done | bytes 524304 | tf_op jit(solution)/shard_map/reduce_scatter | solution.py:143
  200.8 38.0 %reduce-scatter.9.cloned.1.call-done = bf16[128,2048]{1,0:T(8,128)(2,1)} async-done(((bf16[512,2048]{1,0:T(8,128)(2,1)}), bf16[128,2048]{1,0:T(8,128)(2,1)}) %reduce-scatter.9.cloned.1.call-update) | async-done | bytes 524304 | tf_op jit(solution)/shard_map/reduce_scatter | solution.py:143
  238.8 38.0 %reduce-scatter.5.cloned.1.call-done = bf16[128,2048]{1,0:T(8,128)(2,1)} async-done(((bf16[512,2048]{1,0:T(8,128)(2,1)}), bf16[128,2048]{1,0:T(8,128)(2,1)}) %reduce-scatter.5.cloned.1.call-update) | async-done | bytes 524304 | tf_op jit(solution)/shard_map/reduce_scatter | solution.py:143
  276.9 38.0 %reduce-scatter.7.cloned.1.call-done = bf16[128,2048]{1,0:T(8,128)(2,1)} async-done(((bf16[512,2048]{1,0:T(8,128)(2,1)}), bf16[128,2048]{1,0:T(8,128)(2,1)}) %reduce-scatter.7.cloned.1.call-update) | async-done | bytes 524304 | tf_op jit(solution)/shard_map/reduce_scatter | solution.py:143
  314.9 3.0 pad_maximum_fusion
  (21 shorter events, 0.6 us)
Async XLA Ops:
  6.5 5.3 %copy-start.1 = (bf16[512,16,128]{2,1,0:T(8,128)(2,1)S(1)}, bf16[512,16,128]{2,1,0:T(8,128)(2,1)}, u32[]{:S(2)}) copy-start(bf16[512,16,128]{2,1,0:T(8,128)(2,1)} %param.7) | copy-start | bytes 6291460
  6.5 36.0 %all-gather.5.cloned.1.call-start = ((), (), s32[]{:S(2)}) async-start(), calls=%async_computation.8 | async-start | bytes 2433024 | tf_op jit(solution)/shard_map/all_gather | solution.py:122
  9.9 62.7 %all-gather.7.cloned.1.call-start = ((), (), s32[]{:S(2)}) async-start(), calls=%async_computation.9 | async-start | bytes 2359296 | tf_op jit(solution)/shard_map/all_gather | solution.py:123
  11.8 189.0 %reduce-scatter.11.cloned.1.call-start = ((), (), s32[]{:S(2)}) async-start(), calls=%async_computation.7 | async-start | bytes 2621440 | tf_op jit(solution)/shard_map/reduce_scatter | solution.py:143
  43.2 29.4 %copy-start = (s32[2]{0:T(128)S(1)}, s32[2]{0:T(128)}, u32[]{:S(2)}) copy-start(s32[2]{0:T(128)} %own.1) | copy-start | bytes 28
  165.9 73.0 %reduce-scatter.9.cloned.1.call-start = ((), (), s32[]{:S(2)}) async-start(), calls=%async_computation.6 | async-start | bytes 2621440 | tf_op jit(solution)/shard_map/reduce_scatter | solution.py:143
  175.0 101.8 %reduce-scatter.5.cloned.1.call-start = ((), (), s32[]{:S(2)}) async-start(), calls=%async_computation.4 | async-start | bytes 2621440 | tf_op jit(solution)/shard_map/reduce_scatter | solution.py:143
  184.3 130.6 %reduce-scatter.7.cloned.1.call-start = ((), (), s32[]{:S(2)}) async-start(), calls=%async_computation.5 | async-start | bytes 2621440 | tf_op jit(solution)/shard_map/reduce_scatter | solution.py:143
Sparse Core Ops, SparseCore 0:
  10.1 32.4 all-gather.4
  44.1 28.5 all-gather.6
  166.0 34.7 reduce-scatter.10
  203.6 35.1 reduce-scatter.8
  241.7 35.1 reduce-scatter.4
  279.7 35.1 reduce-scatter.6
where the time goes:
time: 325 us
  waiting for transfers between devices  176 us (54%)
  Pallas kernels  84.1 us (26%)
  matrix products  36.5 us (11%)
  between operations  13.5 us (4%)
  local copies, waits for them, and re-layouts  8.89 us (3%)
  other arithmetic  5.69 us (2%)
    reduce_scatter x4, waiting for transfers between devices, body(): lax.psum_scatter(term, 'head', scatter_dimension=0, tiled=True)  121 us
    pallas_call x1, Pallas kernels, attend(): pl.pallas_call(functools.partial(attend_kernel, per_group, block_len, hea...  84.1 us
    dot_general x4, matrix products, body(): jnp.dot(attended, out_weight[:, c * step:(c + 1) * step], preferred_eleme...  36.5 us
    all_gather x1, waiting for transfers between devices, body(): all_keys = lax.all_gather(key_part, 'ctx', axis=0, tiled=False)  28.8 us
    all_gather x1, waiting for transfers between devices, body(): lax.all_gather(values.reshape(rows, width).T, 'ctx', axis=0, tiled=False)  25.7 us
  transfers between devices with their start and end apart: 6, of which 6 were waited for; matrix products, arithmetic and copies ran while one was open for 11% of the time, Pallas kernels for 0%

commit v1 on v0

v1 whole, which is shorter than its diff:
```python
import functools
import math

import jax
import jax.numpy as jnp
from jax import lax
from jax.experimental import pallas as pl
from jax.experimental.pallas import tpu as pltpu
from jax.sharding import PartitionSpec as P

masked_value = -1e30
COLUMN_STEP = 512
LAG = 3


def attend_kernel(
    per_group, block_len, head_dim, blocks, first_slot, later,
    order, own, key_gain, value_gain,
    q_ref, k_ref, vt_ref, *refs,
):
    group = pl.program_id(0)
    if later:
        old_max, old_total, old_sum, o_ref, max_ref, total_ref, sum_ref = refs
    elif first_slot == 0:
        o_ref, max_ref, total_ref, sum_ref = refs
    else:
        max_ref, total_ref, sum_ref = refs
    place = own[first_slot]

    def tile(index, diagonal, fresh):
        block = order[index]
        owner = lax.div(block, 2)
        key = k_ref[owner]
        value_t = vt_ref[owner]
        gain = key_gain[group * blocks + block]
        scale = value_gain[group * blocks + block]
        if diagonal:
            shape = (block_len, block_len)
            visible = lax.broadcasted_iota(jnp.int32, shape, 0) <= lax.broadcasted_iota(
                jnp.int32, shape, 1
            )
        for h in range(per_group):
            columns = slice(h * head_dim, (h + 1) * head_dim)
            scores = lax.dot_general(
                key, q_ref[:, columns], (((1,), (1,)), ((), ())),
                preferred_element_type=jnp.float32,
            )
            if diagonal:
                scores = jnp.where(visible, scores, masked_value)
            top = jnp.max(scores, axis=0, keepdims=True) * gain
            if not fresh:
                old = max_ref[h : h + 1, :]
                top = jnp.maximum(old, top)
            weights = jnp.exp2(scores * gain - top)
            total = jnp.sum(weights, axis=0, keepdims=True)
            product = lax.dot_general(
                value_t, weights.astype(jnp.bfloat16), (((1,), (0,)), ((), ())),
                preferred_element_type=jnp.float32,
            ) * scale
            if not fresh:
                factor = jnp.exp2(old - top)
                total = total + factor * total_ref[h : h + 1, :]
                product = product + factor * sum_ref[h]
            max_ref[h : h + 1, :] = top
            total_ref[h : h + 1, :] = total
            sum_ref[h] = product

    half = blocks // 2
    if later:
        max_ref[...] = old_max[...]
        total_ref[...] = old_total[...]
        sum_ref[...] = old_sum[...]
        tile(place, True, False)
        start, stop = half, place
    elif first_slot == 0:
        tile(place, True, True)
        start, stop = 0, place
    else:
        tile(0, False, True)
        start, stop = 1, half

    @pl.loop(start, stop)
    def _(index):
        tile(index, False, False)

    if later or first_slot == 0:
        for h in range(per_group):
            columns = slice(h * head_dim, (h + 1) * head_dim)
            mean = sum_ref[h] / total_ref[h : h + 1, :]
            o_ref[:, columns] = mean.T.astype(o_ref.dtype)


def attend(facts, query, gathered, group_count, head_dim, slot, state=None):
    rows, width = query.shape
    devices = gathered.shape[0]
    block_len = rows // 2
    group_width = width // group_count
    per_group = group_width // head_dim
    heads = group_count * per_group
    blocks = facts[0].shape[0]
    later = state is not None
    tiles = blocks // 4 if later or slot == 0 else blocks // 2
    pairs = tiles * block_len * block_len * heads
    row_spec = pl.BlockSpec((per_group, block_len), lambda g, *_: (g, 0))
    sum_spec = pl.BlockSpec((per_group, head_dim, block_len), lambda g, *_: (g, 0, 0))
    state_specs = [row_spec, row_spec, sum_spec]
    row_shape = (per_group, block_len)
    sum_shape = (per_group, head_dim, block_len)
    first_value = block_len // head_dim
    outs = ([pl.BlockSpec((block_len, group_width), lambda g, *_: (0, g))],
            [jax.ShapeDtypeStruct((block_len, width), jnp.bfloat16)])
    scratch = [
        pltpu.VMEM(row_shape, jnp.float32),
        pltpu.VMEM(row_shape, jnp.float32),
        pltpu.VMEM(sum_shape, jnp.float32),
    ]
    if not later and slot == 1:
        outs = (state_specs, [
            jax.ShapeDtypeStruct((heads, block_len), jnp.float32),
            jax.ShapeDtypeStruct((heads, block_len), jnp.float32),
            jax.ShapeDtypeStruct((heads, head_dim, block_len), jnp.float32),
        ])
        scratch = []
    results = pl.pallas_call(
        functools.partial(
            attend_kernel, per_group, block_len, head_dim, blocks, slot, later
        ),
        grid_spec=pltpu.PrefetchScalarGridSpec(
            num_scalar_prefetch=4,
            grid=(group_count,),
            in_specs=[
                pl.BlockSpec((block_len, group_width), lambda g, *_: (slot, g)),
                pl.BlockSpec((devices, block_len, head_dim), lambda g, *_: (0, 0, g)),
                pl.BlockSpec(
                    (devices, head_dim, block_len), lambda g, *_: (0, first_value + g, 0)
                ),
            ] + (state_specs if later else []),
            out_specs=outs[0],
            scratch_shapes=scratch,
        ),
        out_shape=outs[1],
        compiler_params=pltpu.CompilerParams(vmem_limit_bytes=40 * 1024 * 1024),
        cost_estimate=pl.CostEstimate(
            flops=4 * pairs * head_dim, bytes_accessed=4 << 20, transcendentals=pairs
        ),
    )(*facts, query, gathered, gathered, *(state if later else ()))
    return results if len(results) > 1 else results[0]


def project_kernel(
    chunks,
    low_ref, high_ref, w_ref, o_ref,
    lhs, sent, kept, arrived, passed, ended,
    send_one, recv_one, send_two, recv_two,
):
    t = pl.program_id(0)
    me = lax.axis_index("head")
    along_x = me + 1 - 2 * (me % 2)
    along_y = (me + 2) % 4
    part = low_ref.shape[0] // 2

    @pl.when(t == 0)
    def _():
        barrier = pltpu.get_barrier_semaphore()
        for partner in (along_x, along_y):
            pl.semaphore_signal(
                barrier, inc=1, device_id={"head": partner},
                device_id_type=pl.DeviceIdType.MESH,
            )
        for parity in range(2):
            near, far = (along_x, along_y) if parity == 0 else (along_y, along_x)
            for slot, owner in enumerate((3 - me, near, far, me)):
                rows = pl.ds(pl.multiple_of((owner % 2) * part, part), part)

                @pl.when(owner // 2 == 0)
                def _():
                    lhs[parity, slot * part : (slot + 1) * part, :] = low_ref[rows, :]

                @pl.when(owner // 2 == 1)
                def _():
                    lhs[parity, slot * part : (slot + 1) * part, :] = high_ref[rows, :]

        pl.semaphore_wait(barrier, 2)

    def first_copy(c):
        near = along_x + (c % 2) * (along_y - along_x)
        return pltpu.make_async_remote_copy(
            src_ref=sent.at[c], dst_ref=arrived.at[c],
            send_sem=send_one.at[c], recv_sem=recv_one.at[c],
            device_id={"head": near}, device_id_type=pl.DeviceIdType.MESH,
        )

    def second_copy(c):
        far = along_y + (c % 2) * (along_x - along_y)
        return pltpu.make_async_remote_copy(
            src_ref=passed.at[c], dst_ref=ended.at[c],
            send_sem=send_two.at[c], recv_sem=recv_two.at[c],
            device_id={"head": far}, device_id_type=pl.DeviceIdType.MESH,
        )

    @pl.when(t < chunks)
    def _():
        term = jnp.dot(lhs[t % 2], w_ref[...], preferred_element_type=jnp.float32)
        term = term.astype(jnp.bfloat16)
        sent[t] = term[: 2 * part]
        kept[t] = term[2 * part :]
        first_copy(t).start()

    @pl.when((t >= LAG) & (t < chunks + LAG))
    def _():
        c = t - LAG
        first_copy(c).wait()
        passed[c] = (
            arrived[c, :part, :].astype(jnp.float32) + kept[c, :part, :].astype(jnp.float32)
        ).astype(jnp.bfloat16)
        second_copy(c).start()

    @pl.when(t >= 2 * LAG)
    def _():
        c = t - 2 * LAG
        second_copy(c).wait()
        o_ref[...] = (
            arrived[c, part:, :].astype(jnp.float32)
            + kept[c, part:, :].astype(jnp.float32)
            + ended[c].astype(jnp.float32)
        ).astype(jnp.bfloat16)


def project(low, high, weight):
    depth, columns = weight.shape
    rows = 2 * low.shape[0]
    part = rows // 4
    step = COLUMN_STEP
    chunks = columns // step
    last = chunks - 1
    return pl.pallas_call(
        functools.partial(project_kernel, chunks),
        grid_spec=pltpu.PrefetchScalarGridSpec(
            num_scalar_prefetch=0,
            grid=(chunks + 2 * LAG,),
            in_specs=[
                pl.BlockSpec((rows // 2, depth), lambda t: (0, 0)),
                pl.BlockSpec((rows // 2, depth), lambda t: (0, 0)),
                pl.BlockSpec((depth, step), lambda t: (0, jnp.minimum(t, last))),
            ],
            out_specs=pl.BlockSpec((part, step), lambda t: (0, jnp.maximum(t - 2 * LAG, 0))),
            scratch_shapes=[
                pltpu.VMEM((2, rows, depth), jnp.bfloat16),
                pltpu.VMEM((chunks, 2 * part, step), jnp.bfloat16),
                pltpu.VMEM((chunks, 2 * part, step), jnp.bfloat16),
                pltpu.VMEM((chunks, 2 * part, step), jnp.bfloat16),
                pltpu.VMEM((chunks, part, step), jnp.bfloat16),
                pltpu.VMEM((chunks, part, step), jnp.bfloat16),
                pltpu.SemaphoreType.DMA((chunks,)),
                pltpu.SemaphoreType.DMA((chunks,)),
                pltpu.SemaphoreType.DMA((chunks,)),
                pltpu.SemaphoreType.DMA((chunks,)),
            ],
        ),
        out_shape=jax.ShapeDtypeStruct((part, columns), jnp.bfloat16),
        compiler_params=pltpu.CompilerParams(
            collective_id=0, has_side_effects=True, vmem_limit_bytes=56 * 1024 * 1024
        ),
        cost_estimate=pl.CostEstimate(
            flops=2 * rows * depth * columns, bytes_accessed=2 * depth * columns,
            transcendentals=0,
        ),
    )(low, high, weight)


def body(query, keys, values, k_scale, v_scale, block_place, out_weight):
    rows, head_count, head_dim = query.shape
    group_count = keys.shape[1]
    slots = block_place.shape[0]
    devices = lax.axis_size("ctx")
    blocks = slots * devices
    block_len = rows // slots
    width = group_count * head_dim
    facts = jnp.concatenate(
        [k_scale, v_scale, block_place[:, None].astype(jnp.bfloat16)], axis=1
    )
    facts = jnp.pad(facts, ((0, 16 - slots), (0, block_len - facts.shape[1])))

    def payload(slot):
        part = slice(slot * block_len, (slot + 1) * block_len)
        key = keys[part].reshape(block_len, width)
        key = jnp.pad(key, ((0, 0), (0, block_len - width))) if width < block_len else key
        return [key, values[part].reshape(block_len, width).T]

    low_part = lax.all_gather(jnp.concatenate(payload(0) + [facts]), "ctx", axis=0)
    high_part = lax.all_gather(jnp.concatenate(payload(1)), "ctx", axis=0)
    base = block_len + width
    all_facts = low_part[:, base : base + slots, : 2 * group_count + 1].reshape(blocks, -1)
    all_facts = all_facts.astype(jnp.float32)
    places = all_facts[:, -1].astype(jnp.int32)
    ids = jnp.arange(blocks, dtype=jnp.int32)
    order = jnp.sum(jnp.where(places[None, :] == ids[:, None], ids[None, :], 0), axis=1)
    rate = math.log2(math.e) / math.sqrt(head_dim)
    key_gain = (all_facts[:, :group_count] * rate).T.reshape(-1)
    value_gain = all_facts[:, group_count : 2 * group_count].T.reshape(-1)
    known = (order, block_place, key_gain, value_gain)
    flat = query.reshape(rows, head_count * head_dim)
    state = attend(known, flat, low_part, group_count, head_dim, 1)
    low = attend(known, flat, low_part, group_count, head_dim, 0)
    high = attend(known, flat, high_part, group_count, head_dim, 1, state)
    if lax.axis_size("head") == 4:
        return project(low, high, out_weight)
    term = jnp.dot(jnp.concatenate([low, high]), out_weight, preferred_element_type=jnp.float32)
    return lax.psum_scatter(
        term.astype(jnp.bfloat16), "head", scatter_dimension=0, tiled=True
    )


def solution(mesh):
    placed = (
        P("ctx", "head", None),
        P("ctx", "head", None),
        P("ctx", "head", None),
        P("ctx", "head"),
        P("ctx", "head"),
        P("ctx"),
        P("head", None),
    )
    return jax.shard_map(
        body, mesh=mesh, in_specs=placed, out_specs=P(("ctx", "head"), None), check_vma=False
    )
```

time: 325 us -> 226 us (0.70)
  waiting for transfers between devices: 176 us -> 29.5 us
  Pallas kernels: 84.1 us -> 162 us
  matrix products: 36.5 us -> 0 us
  local copies, waits for them, and re-layouts: 8.89 us -> 17 us
    reduce_scatter x4 -> x0, waiting for transfers between devices: 121 us -> none  [body(): lax.psum_scatter(term, 'head', scatter_dimension=0, tiled=True)]
    pallas_call x0 -> x1, Pallas kernels: none -> 77.3 us  [project(): pl.pallas_call(functools.partial(project_kernel, chunks), grid_spec=pltpu...]
    dot_general x4 -> x0, matrix products: 36.5 us -> none  [body(): jnp.dot(attended, out_weight[:, c * step:(c + 1) * step], preferred_eleme...]
    all_gather x2, waiting for transfers between devices: 54.4 us -> 29.5 us  [the longest x1 29.5 us: body(): lax.all_gather(jnp.concatenate(payload(0) + [facts]), 'ctx', axis=0)]
    unnamed x6 -> x18, local copies, waits for them, and re-layouts: 2.85 us -> 13.3 us
    pallas_call x1 -> x3, Pallas kernels: 84.1 us -> 84.9 us  [attend(): pl.pallas_call(functools.partial(attend_kernel, per_group, block_len, hea...]
  transfers between devices with their start and end apart: 6 -> 2, of which waited for: 6 -> 1; matrix products, arithmetic and copies ran while one was open for 11% -> 2% of each run, Pallas kernels for 0% -> 33%
where the time goes in v1:
time: 226 us
  Pallas kernels  162 us (72%)
  waiting for transfers between devices  29.5 us (13%)
  local copies, waits for them, and re-layouts  17 us (8%)
  between operations  13.5 us (6%)
  other arithmetic  3.25 us (1%)
    pallas_call x3, Pallas kernels, attend(): pl.pallas_call(functools.partial(attend_kernel, per_group, block_len, hea...  84.9 us
    pallas_call x1, Pallas kernels, project(): pl.pallas_call(functools.partial(project_kernel, chunks), grid_spec=pltpu...  77.3 us
    all_gather x1, waiting for transfers between devices, body(): lax.all_gather(jnp.concatenate(payload(0) + [facts]), 'ctx', axis=0)  29.5 us
    unnamed x18, local copies, waits for them, and re-layouts  13.3 us
  transfers between devices with their start and end apart: 2, of which 1 were waited for; matrix products, arithmetic and copies ran while one was open for 2% of the time, Pallas kernels for 33%

profile of v1, /device:TPU:0, one launch (start us, length us, event | category | flops | bytes accessed | tf_op | source)
XLA Modules:
  0.0 225.5 jit_solution(18402533980997746076)
XLA Ops:
  6.5 1.1 fusion.12
  7.7 0.1 copy.23
  7.8 1.2 fusion.11
  9.0 0.7 convert_bitcast_fusion
  9.7 0.1 copy.19
  9.8 0.7 fusion.8
  10.5 0.7 pad_maximum_fusion
  11.5 0.7 pad_maximum_fusion.1
  12.2 2.1 copy.31
  14.4 29.5 %all-gather.5.cloned.1.call-done = bf16[4224,256]{1,0:T(8,128)(2,1)} async-done(((bf16[528,256]{1,0:T(8,128)(2,1)}), bf16[4224,256]{1,0:T(8,128)(2,1)}) %all-gather.5.cloned.1.call-update) | async-done | bytes 2162704 | tf_op jit(solution)/shard_map/all_gather | solution.py:290
  43.8 0.7 slice.32
  45.0 0.2 fusion.10
  45.2 0.1 select_reduce_fusion.order
  45.3 1.6 copy-done.5
  46.9 34.6 %shard_map.73.low_ref = bf16[256,2048]{1,0:T(8,128)(2,1)S(1)} custom-call(s32[16]{0:T(128)S(1)} %select_reduce_fusion.order, s32[2]{0:T(128)S(1)} %copy-done.4, f32[32]{0:T(128)S(1)} %reshape.33.key_gain, f32[32]{0:T(128)S(1)} %reshape.34.value_gain, bf16[512,2048]{1,0:T(8,128)(2,1)S(1)} %bitcast.28, bf16[8,528,256]{2,1,0:T(8,128)(2,1)S(1)} %bitcast.34, ...), custom_call_target="tpu_custom_call" | custom-call | flops 2147483648 | bytes 4194304 | tf_op jit(solution)/shard_map/pallas_call | solution.py:124
  81.5 1.0 copy-done.6
  82.5 39.1 %shard_map.74 = (f32[16,256]{1,0:T(8,128)S(1)}, f32[16,256]{1,0:T(8,128)S(1)}, f32[16,128,256]{2,1,0:T(8,128)S(1)}) custom-call(s32[16]{0:T(128)S(1)} %select_reduce_fusion.order, s32[2]{0:T(128)S(1)} %copy-done.4, f32[32]{0:T(128)S(1)} %reshape.33.key_gain, f32[32]{0:T(128)S(1)} %reshape.34.value_gain, bf16[512,2048]{1,0:T(8,128)(2,1)S(1)} %bitcast.29, ...), custom_call_target="tpu_custom_call" | custom-call | flops 4294967296 | bytes 4194304 | tf_op jit(solution)/shard_map/pallas_call | solution.py:124
  121.6 1.3 copy-done.1
  122.9 1.6 copy-done
  124.5 1.6 copy-done.2
  126.1 11.2 %shard_map.75.high_ref = bf16[256,2048]{1,0:T(8,128)(2,1)S(1)} custom-call(s32[16]{0:T(128)S(1)} %select_reduce_fusion.order, s32[2]{0:T(128)S(1)} %copy-done.4, f32[32]{0:T(128)S(1)} %reshape.33.key_gain, f32[32]{0:T(128)S(1)} %reshape.34.value_gain, bf16[512,2048]{1,0:T(8,128)(2,1)S(1)} %bitcast.30, bf16[8,512,256]{2,1,0:T(8,128)(2,1)S(1)} %bitcast.31, ...), custom_call_target="tpu_custom_call" | custom-call | flops 2147483648 | bytes 4194304 | tf_op jit(solution)/shard_map/pallas_call | solution.py:124
  137.3 1.0 copy-done.3
  138.3 77.3 %shard_map.76 = bf16[128,8192]{1,0:T(8,128)(2,1)} custom-call(bf16[256,2048]{1,0:T(8,128)(2,1)} %copy-done.6, bf16[256,2048]{1,0:T(8,128)(2,1)} %copy-done.3, bf16[2048,8192]{1,0:T(8,128)(2,1)} %w_ref.1), custom_call_target="tpu_custom_call" | custom-call | flops 17179869184 | bytes 33554432 | tf_op jit(solution)/shard_map/pallas_call | solution.py:236
  215.6 3.1 %copy.35 = bf16[128,8192]{1,0:T(8,128)(2,1)} copy(bf16[128,8192]{1,0:T(8,128)(2,1)} %shard_map.76) | data formatting | bytes 4194304
  (22 shorter events, 0.7 us)
Async XLA Ops:
  6.5 37.3 %all-gather.5.cloned.1.call-start = ((), (), s32[]{:S(2)}) async-start(), calls=%async_computation | async-start | bytes 2433024 | tf_op jit(solution)/shard_map/all_gather | solution.py:290
  11.3 111.7 %all-gather.7.cloned.1.call-start = ((), (), s32[]{:S(2)}) async-start(), calls=%async_computation.1 | async-start | bytes 2359296 | tf_op jit(solution)/shard_map/all_gather | solution.py:291
  12.2 33.1 %copy-start.4 = (s32[2]{0:T(128)S(1)}, s32[2]{0:T(128)}, u32[]{:S(2)}) copy-start(s32[2]{0:T(128)} %own.5) | copy-start | bytes 28
  45.3 1.6 copy-start.5
  81.5 1.0 copy-start.6
  121.6 1.3 copy-start.1
  122.9 1.6 copy-start
  124.5 1.6 copy-start.2
  137.3 1.0 copy-start.3
Sparse Core Ops, SparseCore 0:
  11.4 32.4 all-gather.4
  45.4 28.6 all-gather.6
